TPU v7x, 256 devices: a whole 4x4x8 slice. The times are simulated.
256 devices in a mesh: chan: 16 (over y, x_lo, core), stn: 16 (over z, x_hi).
Axes of the slice: x: 4 (x_hi: 2, x_lo: 2; x = x_hi * 2 + x_lo), y: 4, z: 8, core: 2. Of those that a mesh axis runs over, the one named last changes fastest.
Arguments:
- voltages: bfloat16 [1024, 196608], P('stn', 'chan'), may hold values from -6 to 6
- pfb_taps: float32 [16, 512], replicated, may hold values from -1.5 to 1.5
- flags: int32 [512, 256, 48], P('stn', 'chan'), may hold values 0 or 1
Outputs:
- visibilities: float32 [256, 2, 1024, 1024], P('chan', None, 'stn')
All inputs are finite; a program needn't handle non-finite values. No bound on the sum of `flags` on one device may be relied on, other than what follows from the above.
Results may differ from a plain program's by a relative error of at most 0.0062.
Values may be sent and summed in bfloat16 or wider, within the bound.
A program may use at most 128 MiB of HBM per device.

v0:
```python
import math

import jax
import jax.numpy as jnp
from jax import lax
from jax.sharding import PartitionSpec as P

POLS = 2


def shifted(block, axis, distance):
    devices = range(lax.axis_size(axis))
    route = [(i - distance, i) for i in devices if i - distance in devices]
    return lax.ppermute(block, axis, route)


def dft_table(length):
    rows_index = jnp.arange(length, dtype=jnp.int32)
    chan_index = rows_index // 2
    sample_index = jnp.arange(length, dtype=jnp.int32)
    phase_step = chan_index[:, None] * sample_index[None, :] % length
    angles = phase_step.astype(jnp.float32) * (2.0 * math.pi / length)
    values = jnp.where((rows_index % 2 == 0)[:, None], jnp.cos(angles), -jnp.sin(angles))
    return (values / math.sqrt(length)).astype(jnp.bfloat16)


def cross_tile(local, remote, count):
    prods = jnp.einsum("cpat,cqbt->cpqab", local, remote, preferred_element_type=jnp.float32)
    real_part = prods[:, 0, 0] + prods[:, 1, 1]
    imag_part = prods[:, 1, 0] - prods[:, 0, 1]
    return jnp.stack([real_part, imag_part], axis=1) / count


def shards(voltages, pfb_taps, flags):
    taps = pfb_taps.shape[0]
    length = pfb_taps.shape[1]
    local_signals = voltages.shape[0]
    spec_local = voltages.shape[1] // length
    frames = voltages.reshape(local_signals, spec_local, length)
    earlier = shifted(frames[:, spec_local - (taps - 1) :, :], "chan", 1)
    padded = jnp.concatenate([earlier, frames], axis=1)
    filtered = jnp.zeros((local_signals, spec_local, length), jnp.float32)
    for tap_index in range(taps):
        offset = taps - 1 - tap_index
        filtered = filtered + pfb_taps[tap_index] * padded[:, offset : offset + spec_local, :]
    filtered = filtered.astype(jnp.bfloat16)
    spectra = jnp.einsum(
        "qn,stn->qst", dft_table(length), filtered, preferred_element_type=jnp.float32
    ).astype(jnp.bfloat16)
    turned = lax.all_to_all(spectra, "chan", split_axis=0, concat_axis=2, tiled=True)
    chan_local = turned.shape[0] // 2
    total = turned.shape[2]
    stations_local = flags.shape[0]
    blocks = flags.shape[2]
    keep = jnp.transpose(flags, (1, 0, 2)).astype(jnp.bfloat16)[:, None, :, None, :, None]
    shaped = turned.reshape(chan_local, 2, stations_local, POLS, blocks, total // blocks)
    weighted = (shaped * keep).reshape(chan_local, 2, local_signals, total)
    count = float(total)
    return cross_tile(weighted, lax.all_gather(weighted, "stn", axis=2, tiled=True), count)


def solution(mesh):
    placed = (P("stn", "chan"), P(), P("stn", "chan", None))
    return jax.shard_map(
        shards, mesh=mesh, in_specs=placed, out_specs=P("chan", None, "stn", None), check_vma=False
    )
```

profile of v0, /device:TPU:4, one launch (start us, length us, event | category | flops | bytes accessed | tf_op | source)
XLA Modules:
  0.0 441.6 jit_solution(7397910083880417498)
XLA Ops:
  6.5 0.0 copy-start.3
  6.5 1.7 copy.45
  8.2 0.1 slice.144
  8.3 1.8 collective-permute-start
  10.1 0.0 copy-done.3
  10.2 2.0 collective-permute-done
  12.2 0.1 constant_dynamic-update-slice_fusion.1
  12.3 0.0 copy-done
  12.3 0.2 constant_dynamic-update-slice_fusion
  12.5 12.0 %convolution_convert_fusion = bf16[512,64,24]{0,1,2:T(8,128)(2,1)} fusion(bf16[64,39,512]{2,0,1:T(8,128)(2,1)S(1)} %constant_dynamic-update-slice_fusion, f32[512]{0:T(512)S(1)} %bitcast.87, f32[512]{0:T(512)S(1)} %bitcast.88, f32[512]{0:T(512)S(1)} %bitcast.74, f32[512]{0:T(512)S(1)} %bitcast.75, f32[512]{0:T(512)S(1)} %bitcast.76, f32[512]{0:T(512)S(1)} %bitcast.77, ...), kind=kOutput, calls=%fused_computation.11 | convolution fusion | flops 848560128 | bytes 26774016 | tf_op jit(solution)/shard_map/qn,stn->qst/dot_general | solution.py:47
  24.5 3.9 copy.26
  28.4 0.0 copy-start.2
  28.4 3.2 reshape.91
  31.6 17.0 %all-to-all-start = ((bf16[16,2,24576]{2,1,0:T(2,128)(2,1)}), bf16[16,2,24576]{2,1,0:T(2,128)(2,1)}, u32[]{:S(2)}, u32[]{:S(2)}) async-start(bf16[16,2,24576]{2,1,0:T(2,128)(2,1)} %reshape.91), calls=%async_computation | async-start | bytes 3145728 | tf_op jit(solution)/shard_map/all_to_all | solution.py:50
  48.7 0.0 all-gather.2.cloned.1.call-start
  48.7 0.0 copy-done.2
  48.8 0.2 copy.28
  49.0 4.3 mul.245
  53.3 6.4 %copy.29 = bf16[16,64,384]{2,1,0:T(8,128)(2,1)} copy(bf16[16,64,384]{0,2,1:T(8,128)(2,1)} %bitcast.65) | data formatting | bytes 1572864 | tf_op jit(solution)/shard_map/mul | solution.py:57
  59.7 11.3 %all-to-all-done = bf16[16,2,24576]{2,1,0:T(2,128)(2,1)} async-done(((bf16[16,2,24576]{2,1,0:T(2,128)(2,1)}), bf16[16,2,24576]{2,1,0:T(2,128)(2,1)}, u32[]{:S(2)}, u32[]{:S(2)}) %all-to-all-start) | async-done | bytes 1572896 | tf_op jit(solution)/shard_map/all_to_all | solution.py:50
  71.0 3.8 reshape.92
  74.8 2.5 copy.27
  77.3 3.3 copy.30
  80.7 0.0 copy-done.1
  80.7 1.3 broadcast_multiply_fusion
  82.0 0.0 all-gather.2.cloned.1.call-update
  82.0 318.0 %all-gather.2.cloned.1.call-done = bf16[16,2,1024,384]{3,2,1,0:T(8,128)(2,1)} async-done(((bf16[16,2,64,384]{3,2,1,0:T(8,128)(2,1)}), bf16[16,2,1024,384]{3,2,1,0:T(8,128)(2,1)}) %all-gather.2.cloned.1.call-update) | async-done | bytes 25165840 | tf_op jit(solution)/shard_map/all_gather | solution.py:59
  400.0 19.7 %fusion.2 = f32[16,2,2,64,1024]{4,3,1,2,0:T(8,128)} fusion(bf16[16,2,1024,384]{3,2,1,0:T(8,128)(2,1)} %all-gather.2.cloned.1.call-done, bf16[16,2,64,384]{3,2,1,0:T(8,128)(2,1)} %broadcast_multiply_fusion), kind=kOutput, calls=%fused_computation.2 | convolution fusion | flops 3221225472 | bytes 43515904 | tf_op jit(solution)/shard_map/cpat,cqbt->cpqab/dot_general | solution.py:28
  419.7 4.4 fusion.5
  424.1 4.4 fusion.7
  428.5 2.0 maximum_multiply_fusion
  430.5 4.2 copy.33
  (6 shorter events, 0.1 us)
Async XLA Ops:
  6.5 3.6 copy-start.3
  6.5 5.8 %copy-start = (bf16[64,12288]{1,0:T(8,128)(2,1)S(1)}, bf16[64,12288]{1,0:T(8,128)(2,1)}, u32[]{:S(2)}) copy-start(bf16[64,12288]{1,0:T(8,128)(2,1)} %param.3) | copy-start | bytes 4718596
  8.3 3.9 collective-permute-start
  28.4 20.3 %copy-start.2 = (s32[32,16,48]{2,1,0:T(8,128)S(1)}, s32[32,16,48]{2,1,0:T(8,128)}, u32[]{:S(2)}) copy-start(s32[32,16,48]{2,1,0:T(8,128)} %param.5) | copy-start | bytes 294916
  31.6 39.4 %all-to-all-start = ((bf16[16,2,24576]{2,1,0:T(2,128)(2,1)}), bf16[16,2,24576]{2,1,0:T(2,128)(2,1)}, u32[]{:S(2)}, u32[]{:S(2)}) async-start(bf16[16,2,24576]{2,1,0:T(2,128)(2,1)} %reshape.91), calls=%async_computation | async-start | bytes 3145728 | tf_op jit(solution)/shard_map/all_to_all | solution.py:50
  48.7 351.3 %all-gather.2.cloned.1.call-start = ((), (), s32[]{:S(2)}) async-start(), calls=%async_computation.1 | async-start | bytes 26738688 | tf_op jit(solution)/shard_map/all_gather | solution.py:59
  77.3 3.3 copy-start.1
Sparse Core Ops, SparseCore 0:
  82.1 317.8 all-gather.1
where the time goes:
time: 445 us; the launch traced here: 442 us
  waiting for transfers between devices  331 us (74%)
  local copies, waits for them, and re-layouts  34 us (8%)
  matrix products  31.7 us (7%)
  starting transfers between devices  18.9 us (4%)
  between operations  13.6 us (3%)
  other arithmetic  12.1 us (3%)
    all_gather x1, waiting for transfers between devices, shards(): lax.all_gather(weighted, 'stn', axis=2, tiled=True)  318 us
    dot_general x1, matrix products, cross_tile(): jnp.einsum('cpat,cqbt->cpqab', local, remote, preferred_element_type=jnp....  19.7 us
    all_to_all x1, starting transfers between devices, shards(): lax.all_to_all(spectra, 'chan', split_axis=0, concat_axis=2, tiled=True)  17 us
    dot_general x1, matrix products, shards(): jnp.einsum('qn,stn->qst', dft_table(length), filtered, preferred_element_...  12 us
    all_to_all x1, waiting for transfers between devices, shards(): lax.all_to_all(spectra, 'chan', split_axis=0, concat_axis=2, tiled=True)  11.3 us
    mul x2, local copies, waits for them, and re-layouts, shards(): weighted = (shaped * keep).reshape(chan_local, 2, local_signals, total)  10.7 us
  transfers between devices with their start and end apart: 3, of which 3 were waited for; matrix products, arithmetic and copies ran while one was open for 2% of the time, Pallas kernels for 0%

commit v1 on v0

v1 whole, which is shorter than its diff:
```python
import functools
import math

import jax
import jax.numpy as jnp
import ml_dtypes
import numpy as np
from jax import lax
from jax.experimental import pallas as pl
from jax.experimental.pallas import tpu as pltpu
from jax.sharding import PartitionSpec as P

POLS = 2
BF16 = jnp.bfloat16
F32 = jnp.float32
MESH = pl.DeviceIdType.MESH


def dft_table(length, chans, stns):
    sample = np.arange(length)
    order = np.arange(length // 2).reshape(chans, stns).T.reshape(-1)
    phase = (order[:, None] * sample[None, :]) % length
    angles = phase.astype(np.float32) * np.float32(2.0 * math.pi / length)
    angles = angles.astype(np.float64)
    values = np.concatenate([np.cos(angles), -np.sin(angles)], axis=0)
    return (values.astype(np.float32) / np.float32(math.sqrt(length))).astype(ml_dtypes.bfloat16)


def spread(stations, blocks, lanes):
    out = np.zeros((blocks, lanes, lanes), np.float32)
    for fb in range(blocks):
        for lane in range(lanes):
            out[fb, fb * stations + (lane % (lanes // 2)) // POLS, lane] = 1.0
    return out.astype(ml_dtypes.bfloat16)


def kernel(
    n,
    v_ref, taps_ref, tab_ref, mask_ref, spread_ref,
    o_ref,
    ext, filt, w32, wb, rz, bb, mk, mx, zy, zt, sb,
    vsem, hsend, hrecv, msend, mrecv, zsend, zrecv, csend, crecv, osend, orecv, lsem,
):
    ci = lax.axis_index("chan")
    sk = lax.axis_index("stn")
    nfft = 512
    halo = 15
    own = v_ref.shape[1] // nfft

    def stn_at(d):
        return lax.rem(sk + d, n)

    def chan_at(d):
        return lax.rem(ci + d, n)

    load = pltpu.make_async_copy(v_ref, ext.at[:, halo * nfft :], vsem)
    load.start()

    bar = pltpu.get_barrier_semaphore()

    @pl.loop(1, n)
    def _(d):
        pl.semaphore_signal(bar, inc=1, device_id={"stn": stn_at(d)}, device_id_type=MESH)
        pl.semaphore_signal(bar, inc=1, device_id={"chan": chan_at(d)}, device_id_type=MESH)

    def fir(fb):
        @pl.loop(0, 16)
        def _(idx):
            s0 = pl.multiple_of((idx // 4) * 16, 16)
            n0 = pl.multiple_of(lax.rem(idx, 4) * 128, 128)
            taps = [taps_ref[pl.ds(k, 1), pl.ds(n0, 128)] for k in range(16)]
            x = [
                ext[pl.ds(s0, 16), pl.ds(pl.multiple_of((fb * 8 + f) * nfft + n0, 128), 128)].astype(F32)
                for f in range(23)
            ]
            for t in range(8):
                acc = taps[0] * x[t + 15]
                for k in range(1, 16):
                    acc = acc + taps[k] * x[t + 15 - k]
                filt[pl.ds(pl.multiple_of(t * 64 + s0, 16), 16), pl.ds(n0, 128)] = acc.astype(BF16)

    def dft(fb):
        for tt in range(2):
            for p in range(2):
                o = lax.dot_general(
                    tab_ref[p * 256 : (p + 1) * 256, :], filt[tt * 256 : (tt + 1) * 256, :],
                    (((1,), (1,)), ((), ())), preferred_element_type=F32,
                )
                for h in range(2):
                    w32[pl.ds(p * 4 + tt * 2 + h, 256, stride=8), :] = o[:, h * 128 : (h + 1) * 128]

        @pl.loop(0, n)
        def _(k):
            rows = w32[pl.ds(pl.multiple_of(k * 128, 128), 128), :]
            wb[fb, k] = rows.reshape(n, 8, 128).astype(BF16)

    def zcopy(fb, d):
        to = stn_at(d)
        return pltpu.make_async_remote_copy(
            wb.at[fb, to], rz.at[fb, sk], zsend.at[fb, d], zrecv.at[fb, d],
            device_id={"stn": to}, device_id_type=MESH,
        )

    def zlocal(fb):
        return pltpu.make_async_copy(wb.at[fb, sk], rz.at[fb, sk], lsem.at[0, fb])

    def ccopy(fb, d):
        to = chan_at(d)
        return pltpu.make_async_remote_copy(
            rz.at[fb, :, to], bb.at[fb, ci], csend.at[fb, d], crecv.at[fb, d],
            device_id={"chan": to}, device_id_type=MESH,
        )

    def clocal(fb):
        return pltpu.make_async_copy(rz.at[fb, :, ci], bb.at[fb, ci], lsem.at[1, fb])

    def mcopy(d):
        to = stn_at(d)
        return pltpu.make_async_remote_copy(
            mask_ref.at[to], mk.at[sk], msend.at[d], mrecv.at[d],
            device_id={"stn": to}, device_id_type=MESH,
        )

    mlocal = pltpu.make_async_copy(mask_ref.at[sk], mk.at[sk], lsem.at[2, 0])

    def hcopy(part):
        first, count = ((8, 7), (0, 8))[part]
        return pltpu.make_async_remote_copy(
            v_ref.at[:, pl.ds((own - halo + first) * nfft, count * nfft)],
            ext.at[:, pl.ds(first * nfft, count * nfft)],
            hsend.at[part], hrecv.at[part],
            device_id={"chan": lax.rem(ci + 1, n)}, device_id_type=MESH,
        )

    def zstart(fb):
        zlocal(fb).start()

        @pl.loop(1, n)
        def _(d):
            zcopy(fb, d).start()

    def cstart(fb):
        zlocal(fb).wait()

        @pl.loop(1, n)
        def _(d):
            zcopy(fb, d).wait_recv()

        clocal(fb).start()

        @pl.loop(1, n)
        def _(d):
            ccopy(fb, d).start()

    def halo_wait(part):
        first, count = ((8, 7), (0, 8))[part]

        @pl.when(ci > 0)
        def _():
            hcopy(part).wait_recv()

        @pl.when(ci == 0)
        def _():
            ext[:, first * nfft : (first + count) * nfft] = jnp.zeros((64, count * nfft), BF16)

    load.wait()
    fir(2)
    pl.semaphore_wait(bar, 2 * (n - 1))

    @pl.when(ci < n - 1)
    def _():
        hcopy(0).start()
        hcopy(1).start()

    mlocal.start()

    @pl.loop(1, n)
    def _(d):
        mcopy(d).start()

    dft(2)
    zstart(2)
    halo_wait(0)
    fir(1)
    dft(1)
    zstart(1)
    halo_wait(1)
    fir(0)
    dft(0)
    zstart(0)

    mlocal.wait()

    @pl.loop(1, n)
    def _(d):
        mcopy(d).wait_recv()

    for fb in range(3):
        mx[fb] = jnp.dot(
            mk[...].reshape(n * n, 128), spread_ref[fb], preferred_element_type=F32
        )

    lane = lax.broadcasted_iota(jnp.int32, (128, 128), 1)
    low = lane < 64
    row = lax.broadcasted_iota(jnp.int32, (n, 8, 128), 1)

    def assemble(fb):
        clocal(fb).wait()

        @pl.loop(1, n)
        def _(d):
            ccopy(fb, d).wait_recv()

        @pl.loop(0, n // 2)
        def _(jp):
            both = []
            for h in range(2):
                j = 2 * jp + h
                data = bb[fb, :, j].astype(F32)
                flag = mx[fb, pl.ds(pl.multiple_of(j * n, n), n), :]
                both.append((data * flag.reshape(n, 1, 128)).reshape(128, 128))
            turned = [pltpu.roll(b, 64, 1) for b in both]
            parts = [jnp.where(low, both[0], turned[1]), jnp.where(low, turned[0], both[1])]
            c0 = pl.multiple_of(jp * 128, 128)
            for h in range(2):
                z = parts[h]
                r0 = h * 384 + fb * 128
                zy[r0 : r0 + 128, pl.ds(c0, 128)] = z.astype(BF16)
                y = pltpu.roll(z.reshape(n, 8, 128), 4, 1)
                y = jnp.where(row < 4, -y, y).reshape(128, 128)
                zy[r0 : r0 + 128, pl.ds(1024 + c0, 128)] = y.astype(BF16)
                zt[pl.ds(c0, 128), r0 : r0 + 128] = z.T.astype(BF16)

    cstart(2)
    cstart(1)
    assemble(2)
    cstart(0)
    assemble(1)
    assemble(0)

    def ocopy(d):
        to = stn_at(d)
        return pltpu.make_async_remote_copy(
            sb.at[to], o_ref.at[sk], osend.at[d], orecv.at[d],
            device_id={"stn": to}, device_id_type=MESH,
        )

    olocal = pltpu.make_async_copy(sb.at[sk], o_ref.at[sk], lsem.at[2, 1])
    scale = 1.0 / (own * n)

    for step in (2, 1, 3, 0):
        g = lax.rem(sk // 4 + step, 4)
        rows = zt[pl.ds(pl.multiple_of(g * 256, 256), 256), :]
        for col in range(8):
            o = jnp.dot(rows, zy[:, col * 256 : (col + 1) * 256], preferred_element_type=F32)
            o = (o * scale).astype(BF16).reshape(4, 64, 256)
            p, c = divmod(col, 4)
            sb[pl.ds(g * 4, 4), p, :, c * 256 : (c + 1) * 256] = o

        @pl.loop(0, 4)
        def _(jj):
            d = lax.rem(g * 4 + jj - sk + n, n)

            @pl.when(d > 0)
            def _():
                ocopy(d).start()

            @pl.when(d == 0)
            def _():
                olocal.start()

    @pl.when(ci < n - 1)
    def _():
        hcopy(0).wait_send()
        hcopy(1).wait_send()

    @pl.loop(1, n)
    def _(d):
        mcopy(d).wait_send()
        for fb in range(3):
            zcopy(fb, d).wait_send()
            ccopy(fb, d).wait_send()

    olocal.wait()

    @pl.loop(1, n)
    def _(d):
        ocopy(d).wait_send()
        ocopy(d).wait_recv()


def shards(voltages, pfb_taps, flags):
    n = lax.axis_size("stn")
    table = jnp.asarray(dft_table(pfb_taps.shape[1], n, n))
    hot = jnp.asarray(spread(flags.shape[0], 3, 128))
    keep = jnp.transpose(flags, (1, 2, 0)).reshape(n, n, 3 * flags.shape[0]).astype(BF16)
    keep = jnp.pad(keep, ((0, 0), (0, 0), (0, 128 - 3 * flags.shape[0])))
    vm = pl.BlockSpec(memory_space=pltpu.VMEM)
    anywhere = pl.BlockSpec(memory_space=pl.ANY)
    dma = pltpu.SemaphoreType.DMA
    rows = pl.pallas_call(
        functools.partial(kernel, n),
        out_shape=jax.ShapeDtypeStruct((n, 2, 64, 1024), BF16),
        in_specs=[anywhere, vm, vm, vm, vm],
        out_specs=anywhere,
        scratch_shapes=[
            pltpu.VMEM((64, 39 * 512), BF16),
            pltpu.VMEM((512, 512), BF16),
            pltpu.VMEM((2048, 128), F32),
            pltpu.VMEM((3, n, n, 8, 128), BF16),
            pltpu.VMEM((3, n, n, 8, 128), BF16),
            pltpu.VMEM((3, n, n, 8, 128), BF16),
            pltpu.VMEM((n, n, 128), BF16),
            pltpu.VMEM((3, n * n, 128), F32),
            pltpu.VMEM((768, 2048), BF16),
            pltpu.VMEM((1024, 768), BF16),
            pltpu.VMEM((n, 2, 64, 1024), BF16),
            dma, dma((2,)), dma((2,)), dma((n,)), dma((n,)), dma((3, n)), dma((3, n)),
            dma((3, n)), dma((3, n)), dma((n,)), dma((n,)), dma((3, 3)),
        ],
        compiler_params=pltpu.CompilerParams(
            collective_id=0, has_side_effects=True, vmem_limit_bytes=56 << 20
        ),
        name="correlate",
    )(voltages, pfb_taps, table, keep, hot)
    return rows.astype(F32)


def solution(mesh):
    placed = (P("stn", "chan"), P(), P("stn", "chan", None))
    return jax.shard_map(
        shards, mesh=mesh, in_specs=placed, out_specs=P("chan", None, "stn", None), check_vma=False
    )
```

time: 445 us -> 173 us (0.39)
  the two profiles are of different devices: /device:TPU:4 before, /device:TPU:47 now
where the time goes in v1:
time: 173 us
  Pallas kernels  164 us (95%)
  other arithmetic  7.63 us (4%)
    pallas_call x1, Pallas kernels, shards(): pl.pallas_call(functools.partial(kernel, n), out_shape=jax.ShapeDtypeStru...  164 us
    convert_element_type x1, other arithmetic, shards(): return rows.astype(F32)  6.66 us

profile of v1, /device:TPU:47, one launch (start us, length us, event | category | flops | bytes accessed | tf_op | source)
XLA Modules:
  0.0 173.1 jit_solution(16307055113741713093)
XLA Ops:
  0.0 1.0 convert_bitcast_fusion
  1.0 0.2 copy.7
  1.2 0.1 convert_element_type.16
  1.3 0.6 pad.4.mask_ref
  2.0 164.4 %correlate.1 = bf16[16,2,64,1024]{3,2,1,0:T(8,128)(2,1)} custom-call(bf16[64,12288]{1,0:T(8,128)(2,1)} %v_ref.1, f32[16,512]{1,0:T(8,128)} %taps_ref.1, bf16[512,512]{1,0:T(8,128)(2,1)} %constant.7.clone.tab_ref, bf16[16,16,128]{2,1,0:T(8,128)(2,1)} %pad.4.mask_ref, bf16[3,128,128]{2,1,0:T(8,128)(2,1)} %constant.8.clone.spread_ref), custom_call_target="tpu_custom_call" | custom-call | tf_op jit(solution)/shard_map/correlate/pallas_call | solution.py:301
  166.4 6.7 %convert_element_type.17 = f32[16,2,64,1024]{3,2,1,0:T(8,128)} convert(bf16[16,2,64,1024]{3,2,1,0:T(8,128)(2,1)} %correlate.1) | non-fusion elementwise | flops 2097152 | bytes 12582912 | tf_op jit(solution)/shard_map/convert_element_type | solution.py:326

commit v2 on v1

v2 whole, which is shorter than its diff:
```python
import functools
import math

import jax
import jax.numpy as jnp
import ml_dtypes
import numpy as np
from jax import lax
from jax.experimental import pallas as pl
from jax.experimental.pallas import tpu as pltpu
from jax.sharding import PartitionSpec as P

POLS = 2
BF16 = jnp.bfloat16
F32 = jnp.float32
MESH = pl.DeviceIdType.MESH


def dft_table(length):
    sample = np.arange(length)
    phase = (np.arange(length // 2)[:, None] * sample[None, :]) % length
    angles = (phase.astype(np.float32) * np.float32(2.0 * math.pi / length)).astype(np.float64)
    values = np.concatenate([np.cos(angles), -np.sin(angles)], axis=0)
    return (values.astype(np.float32) / np.float32(math.sqrt(length))).astype(ml_dtypes.bfloat16)


def spread(stations, blocks, lanes):
    out = np.zeros((blocks, lanes, lanes), np.float32)
    for fb in range(blocks):
        for lane in range(lanes):
            out[fb, fb * stations + (lane % (lanes // 2)) // POLS, lane] = 1.0
    return out.astype(ml_dtypes.bfloat16)


def kernel(
    n,
    v_ref, taps_ref, tab_ref, mask_ref, spread_ref,
    o_ref,
    ext, filt, w32, wb, rx, mk, mx, zo, lt, zr, ob, mb,
    vsem, hsend, hrecv, msend, mrecv, xsend, xrecv, zsend, zrecv, osend, orecv, bsend, brecv, lsem, olsem,
):
    ci = lax.axis_index("chan")
    sk = lax.axis_index("stn")
    nfft = 512
    halo = 15
    own = v_ref.shape[1] // nfft
    planes = n // 2
    z = sk // 2
    h = lax.rem(sk, 2)

    def at(dz, hh):
        return lax.rem(z + dz + planes, planes) * 2 + hh

    load = pltpu.make_async_copy(v_ref, ext.at[:, halo * nfft :], vsem)
    load.start()

    bar = pltpu.get_barrier_semaphore()

    def greet(chan, stn):
        pl.semaphore_signal(bar, inc=1, device_id={"chan": chan, "stn": stn}, device_id_type=MESH)

    @pl.loop(1, 2 * n)
    def _(e):
        greet(lax.rem(ci + e // 2, n), z * 2 + lax.rem(h + e, 2))

    @pl.loop(0, 2)
    def _(hh):
        for dz in (1, -1, 2, -2, 3, -3):
            greet(ci, at(dz, hh))

    def fir(fb):
        @pl.loop(0, 16)
        def _(idx):
            s0 = pl.multiple_of((idx // 4) * 16, 16)
            n0 = pl.multiple_of(lax.rem(idx, 4) * 128, 128)
            taps = [taps_ref[pl.ds(k, 1), pl.ds(n0, 128)] for k in range(16)]
            x = [
                ext[pl.ds(s0, 16), pl.ds(pl.multiple_of((fb * 8 + f) * nfft + n0, 128), 128)].astype(F32)
                for f in range(23)
            ]
            for t in range(8):
                acc = taps[0] * x[t + 15]
                for k in range(1, 16):
                    acc = acc + taps[k] * x[t + 15 - k]
                filt[pl.ds(pl.multiple_of(t * 64 + s0, 16), 16), pl.ds(n0, 128)] = acc.astype(BF16)

    def dft(fb):
        for tt in range(2):
            for p in range(2):
                o = lax.dot_general(
                    tab_ref[p * 256 : (p + 1) * 256, :], filt[tt * 256 : (tt + 1) * 256, :],
                    (((1,), (1,)), ((), ())), preferred_element_type=F32,
                )
                for half in range(2):
                    w32[pl.ds(p * 4 + tt * 2 + half, 256, stride=8), :] = o[:, half * 128 : (half + 1) * 128]

        @pl.loop(0, n)
        def _(i):
            rows = w32[pl.ds(pl.multiple_of(i * 128, 128), 128), :]
            wb[fb, i] = rows.reshape(2, n // 2, 8, 128).astype(BF16)

    def xcopy(fb, e):
        chan = lax.rem(ci + e // 2, n)
        hh = lax.rem(h + e, 2)
        return pltpu.make_async_remote_copy(
            wb.at[fb, chan, hh], rx.at[fb, h, ci], xsend.at[fb, e], xrecv.at[fb, e],
            device_id={"chan": chan, "stn": z * 2 + hh}, device_id_type=MESH,
        )

    def xlocal(fb):
        return pltpu.make_async_copy(wb.at[fb, ci, h], rx.at[fb, h, ci], lsem.at[fb])

    mcopy = pltpu.make_async_remote_copy(
        mask_ref.at[1 - h], mk.at[h], msend, mrecv,
        device_id={"chan": ci, "stn": z * 2 + 1 - h}, device_id_type=MESH,
    )
    mlocal = pltpu.make_async_copy(mask_ref.at[h], mk.at[h], lsem.at[3])

    def hcopy(part):
        first, count = ((8, 7), (0, 8))[part]
        return pltpu.make_async_remote_copy(
            v_ref.at[:, pl.ds((own - halo + first) * nfft, count * nfft)],
            ext.at[:, pl.ds(first * nfft, count * nfft)],
            hsend.at[part], hrecv.at[part],
            device_id={"chan": lax.rem(ci + 1, n), "stn": sk}, device_id_type=MESH,
        )

    def xstart(fb):
        xlocal(fb).start()

        @pl.loop(1, 2 * n)
        def _(e):
            xcopy(fb, e).start()

    def halo_wait(part):
        first, count = ((8, 7), (0, 8))[part]

        @pl.when(ci > 0)
        def _():
            hcopy(part).wait_recv()

        @pl.when(ci == 0)
        def _():
            ext[:, first * nfft : (first + count) * nfft] = jnp.zeros((64, count * nfft), BF16)

    lane = lax.broadcasted_iota(jnp.int32, (128, 128), 1)
    low = lane < 64
    row = lax.broadcasted_iota(jnp.int32, (n, 8, 128), 1)

    def zcopy(way, s, fb):
        src = zo.at[pl.ds(way * 4, 4)] if s == 0 else zr.at[way, s - 1]
        part = pl.ds(fb * 256, 256)
        return pltpu.make_async_remote_copy(
            src.at[:, part, :], zr.at[way, s, :, part, :], zsend.at[way, s, fb], zrecv.at[way, s, fb],
            device_id={"chan": ci, "stn": at(1 - 2 * way, h)}, device_id_type=MESH,
        )

    def assemble(fb):
        xlocal(fb).wait()

        @pl.loop(1, 2 * n)
        def _(e):
            xcopy(fb, e).wait_recv()

        @pl.loop(0, 8)
        def _(q):
            both = []
            for hh in range(2):
                data = rx[fb, hh, :, q].astype(F32)
                flag = mx[fb, pl.ds(pl.multiple_of((hh * 8 + q) * n, n), n), :]
                both.append((data * flag.reshape(n, 1, 128)).reshape(128, 128))
            turned = [pltpu.roll(b, 64, 1) for b in both]
            zo[q, fb * 256 : fb * 256 + 128, :] = jnp.where(low, both[0], turned[1]).astype(BF16)
            zo[q, fb * 256 + 128 : fb * 256 + 256, :] = jnp.where(low, turned[0], both[1]).astype(BF16)

        for way in range(2):
            zcopy(way, 0, fb).start()

    def turn(fb):
        @pl.loop(0, 8)
        def _(q):
            for part in range(2):
                r0 = fb * 256 + part * 128
                b = zo[q, r0 : r0 + 128, :].astype(F32)
                y = pltpu.roll(b.reshape(n, 8, 128), 4, 1)
                y = jnp.where(row < 4, y, -y).reshape(128, 128)
                lt[q, 0:128, r0 : r0 + 128] = b.T.astype(BF16)
                lt[q, 128:256, r0 : r0 + 128] = y.T.astype(BF16)

    load.wait()
    fir(2)
    dft(2)
    pl.semaphore_wait(bar, 2 * n - 1 + 12)

    @pl.when(ci < n - 1)
    def _():
        hcopy(0).start()

    mlocal.start()
    mcopy.start()
    xstart(2)

    @pl.when(ci < n - 1)
    def _():
        hcopy(1).start()

    mlocal.wait()
    mcopy.wait_recv()
    for fb in range(3):
        mx[fb] = jnp.dot(mk[...].reshape(n * n, 128), spread_ref[fb], preferred_element_type=F32)

    halo_wait(0)
    fir(1)
    dft(1)
    xstart(1)
    assemble(2)
    halo_wait(1)
    fir(0)
    dft(0)
    xstart(0)
    assemble(1)
    turn(2)
    assemble(0)
    turn(1)
    turn(0)

    scale = 1.0 / (own * n)

    def home(way):
        return pl.ds(h * 8 + way * 4, 4)

    def lanes(dz):
        return pl.ds(pl.multiple_of(lax.rem(z + dz + planes, planes) * 128, 128), 128)

    def shift(way, s):
        return s if way == 1 else -s

    def olocal(way, s):
        return pltpu.make_async_copy(
            ob.at[way, s, h], o_ref.at[home(way), :, :, lanes(shift(way, s))], olsem.at[way, s]
        )

    def ocopy(way, s):
        return pltpu.make_async_remote_copy(
            ob.at[way, s, 1 - h], o_ref.at[home(way), :, :, lanes(shift(way, s))],
            osend.at[way, s], orecv.at[way, s],
            device_id={"chan": ci, "stn": z * 2 + 1 - h}, device_id_type=MESH,
        )

    def bcopy(way, s, hh):
        return pltpu.make_async_remote_copy(
            mb.at[way, s - 1, hh], o_ref.at[home(way), :, :, lanes(0)],
            bsend.at[way, s - 1, hh], brecv.at[way, s - 1, h],
            device_id={"chan": ci, "stn": at(shift(way, s), hh)}, device_id_type=MESH,
        )

    def correlate(way, s):
        @pl.loop(0, 4)
        def _(q):
            block = zo[way * 4 + q] if s == 0 else zr[way, s - 1, q]
            o = jnp.dot(lt[way * 4 + q], block, preferred_element_type=F32) * scale
            rows = o.astype(BF16).reshape(2, 2, 64, 128)
            for p in range(2):
                for hh in range(2):
                    ob[way, s, hh, q, p] = rows[p, hh]
            if 0 < s < 4:
                back = (o[0:128].T.astype(BF16), (-o[128:256]).T.astype(BF16))
                for p in range(2):
                    for hh in range(2):
                        mb[way, s - 1, hh, q, p] = back[p][hh * 64 : (hh + 1) * 64]

        olocal(way, s).start()
        ocopy(way, s).start()
        if 0 < s < 4:
            bcopy(way, s, 0).start()
            bcopy(way, s, 1).start()

    for s in range(5):
        if s > 0:
            for fb in (2, 1, 0):
                for way in range(2):
                    zcopy(way, s - 1, fb).wait_recv()
                    if s < 4:
                        zcopy(way, s, fb).start()
        correlate(0, s)
        correlate(1, s)

    @pl.when(ci < n - 1)
    def _():
        hcopy(0).wait_send()
        hcopy(1).wait_send()

    mcopy.wait_send()

    @pl.loop(1, 2 * n)
    def _(e):
        for fb in range(3):
            xcopy(fb, e).wait_send()

    for way in range(2):
        for s in range(4):
            for fb in range(3):
                zcopy(way, s, fb).wait_send()
        for s in range(5):
            olocal(way, s).wait()
            ocopy(way, s).wait_send()
            ocopy(way, s).wait_recv()
        for s in range(1, 4):
            for hh in range(2):
                bcopy(way, s, hh).wait_send()
                pltpu.make_async_remote_copy(
                    mb.at[way, s - 1, hh], o_ref.at[home(way), :, :, lanes(0)],
                    bsend.at[way, s - 1, hh], brecv.at[way, s - 1, hh],
                    device_id={"chan": ci, "stn": at(shift(way, s), hh)}, device_id_type=MESH,
                ).wait_recv()


def shards(voltages, pfb_taps, flags):
    n = lax.axis_size("stn")
    table = jnp.asarray(dft_table(pfb_taps.shape[1]))
    hot = jnp.asarray(spread(flags.shape[0], 3, 128))
    keep = jnp.transpose(flags, (1, 2, 0)).reshape(n, n, 3 * flags.shape[0]).astype(BF16)
    keep = jnp.pad(keep, ((0, 0), (0, 0), (0, 128 - 3 * flags.shape[0]))).reshape(2, n // 2, n, 128)
    vm = pl.BlockSpec(memory_space=pltpu.VMEM)
    anywhere = pl.BlockSpec(memory_space=pl.ANY)
    dma = pltpu.SemaphoreType.DMA
    rows = pl.pallas_call(
        functools.partial(kernel, n),
        out_shape=jax.ShapeDtypeStruct((n, 2, 64, 1024), BF16),
        in_specs=[anywhere, vm, vm, vm, vm],
        out_specs=anywhere,
        scratch_shapes=[
            pltpu.VMEM((64, 39 * 512), BF16),
            pltpu.VMEM((512, 512), BF16),
            pltpu.VMEM((2048, 128), F32),
            pltpu.VMEM((3, n, 2, n // 2, 8, 128), BF16),
            pltpu.VMEM((3, 2, n, n // 2, 8, 128), BF16),
            pltpu.VMEM((2, n // 2, n, 128), BF16),
            pltpu.VMEM((3, n * n, 128), F32),
            pltpu.VMEM((8, 768, 128), BF16),
            pltpu.VMEM((8, 256, 768), BF16),
            pltpu.VMEM((2, 4, 4, 768, 128), BF16),
            pltpu.VMEM((2, 5, 2, 4, 2, 64, 128), BF16),
            pltpu.VMEM((2, 3, 2, 4, 2, 64, 128), BF16),
            dma, dma((2,)), dma((2,)), dma, dma, dma((3, 2 * n)), dma((3, 2 * n)),
            dma((2, 4, 3)), dma((2, 4, 3)), dma((2, 5)), dma((2, 5)),
            dma((2, 3, 2)), dma((2, 3, 2)), dma((4,)), dma((2, 5)),
        ],
        compiler_params=pltpu.CompilerParams(
            collective_id=0, has_side_effects=True, vmem_limit_bytes=56 << 20
        ),
        name="correlate",
    )(voltages, pfb_taps, table, keep, hot)
    return rows.astype(F32)


def solution(mesh):
    placed = (P("stn", "chan"), P(), P("stn", "chan", None))
    return jax.shard_map(
        shards, mesh=mesh, in_specs=placed, out_specs=P("chan", None, "stn", None), check_vma=False
    )
```

time: 173 us -> 150 us (0.87)
  the two profiles are of different devices: /device:TPU:47 before, /device:TPU:4 now
where the time goes in v2:
time: 150 us; the launch traced here: 149 us
  Pallas kernels  140 us (93%)
  other arithmetic  7.63 us (5%)
    pallas_call x1, Pallas kernels, shards(): pl.pallas_call(functools.partial(kernel, n), out_shape=jax.ShapeDtypeStru...  140 us
    convert_element_type x1, other arithmetic, shards(): return rows.astype(F32)  6.66 us

profile of v2, /device:TPU:4, one launch (start us, length us, event | category | flops | bytes accessed | tf_op | source)
XLA Modules:
  0.0 149.0 jit_solution(11470493582675211093)
XLA Ops:
  0.0 1.0 convert_bitcast_fusion
  1.0 0.2 copy.6
  1.2 0.1 convert_element_type.16
  1.3 0.6 pad.4
  2.0 140.3 %correlate.1 = bf16[16,2,64,1024]{3,2,1,0:T(8,128)(2,1)} custom-call(bf16[64,12288]{1,0:T(8,128)(2,1)} %v_ref.1, f32[16,512]{1,0:T(8,128)} %taps_ref.1, bf16[512,512]{1,0:T(8,128)(2,1)} %constant.7.clone.tab_ref, bf16[2,8,16,128]{3,2,1,0:T(8,128)(2,1)} %bitcast.3, bf16[3,128,128]{2,1,0:T(8,128)(2,1)} %constant.8.clone.spread_ref), custom_call_target="tpu_custom_call" | custom-call | tf_op jit(solution)/shard_map/correlate/pallas_call | solution.py:327
  142.3 6.7 %convert_element_type.17 = f32[16,2,64,1024]{3,2,1,0:T(8,128)} convert(bf16[16,2,64,1024]{3,2,1,0:T(8,128)(2,1)} %correlate.1) | non-fusion elementwise | flops 2097152 | bytes 12582912 | tf_op jit(solution)/shard_map/convert_element_type | solution.py:354

commit v3 on v2

--- a/solution.py
+++ b/solution.py
@@ -25,7 +25,7 @@
 
 
 def spread(stations, blocks, lanes):
-    out = np.zeros((blocks, lanes, lanes), np.float32)
+    out = np.zeros((blocks, blocks * stations, lanes), np.float32)
     for fb in range(blocks):
         for lane in range(lanes):
             out[fb, fb * stations + (lane % (lanes // 2)) // POLS, lane] = 1.0
@@ -192,36 +192,43 @@
     dft(2)
     pl.semaphore_wait(bar, 2 * n - 1 + 12)
 
+    mlocal.start()
+    mcopy.start()
+    xstart(2)
+
     @pl.when(ci < n - 1)
     def _():
         hcopy(0).start()
-
-    mlocal.start()
-    mcopy.start()
-    xstart(2)
-
-    @pl.when(ci < n - 1)
-    def _():
         hcopy(1).start()
 
     mlocal.wait()
     mcopy.wait_recv()
     for fb in range(3):
-        mx[fb] = jnp.dot(mk[...].reshape(n * n, 128), spread_ref[fb], preferred_element_type=F32)
-
+        mx[fb] = jnp.dot(mk[...].reshape(n * n, mk.shape[3]), spread_ref[fb], preferred_element_type=F32)
+
+    def pass_on(s, fb):
+        for way in range(2):
+            zcopy(way, s, fb).wait_recv()
+            if s < 3:
+                zcopy(way, s + 1, fb).start()
+
+    assemble(2)
     halo_wait(0)
     fir(1)
     dft(1)
     xstart(1)
-    assemble(2)
+    pass_on(0, 2)
     halo_wait(1)
     fir(0)
     dft(0)
     xstart(0)
+    turn(2)
+    pass_on(1, 2)
     assemble(1)
-    turn(2)
+    turn(1)
+    pass_on(0, 1)
+    pass_on(2, 2)
     assemble(0)
-    turn(1)
     turn(0)
 
     scale = 1.0 / (own * n)
@@ -275,15 +282,23 @@
             bcopy(way, s, 0).start()
             bcopy(way, s, 1).start()
 
-    for s in range(5):
-        if s > 0:
-            for fb in (2, 1, 0):
-                for way in range(2):
-                    zcopy(way, s - 1, fb).wait_recv()
-                    if s < 4:
-                        zcopy(way, s, fb).start()
+    def step(s):
         correlate(0, s)
         correlate(1, s)
+
+    pass_on(1, 1)
+    step(0)
+    pass_on(0, 0)
+    step(1)
+    pass_on(3, 2)
+    pass_on(2, 1)
+    pass_on(1, 0)
+    step(2)
+    pass_on(3, 1)
+    pass_on(2, 0)
+    step(3)
+    pass_on(3, 0)
+    step(4)
 
     @pl.when(ci < n - 1)
     def _():
@@ -320,22 +335,22 @@
     table = jnp.asarray(dft_table(pfb_taps.shape[1]))
     hot = jnp.asarray(spread(flags.shape[0], 3, 128))
     keep = jnp.transpose(flags, (1, 2, 0)).reshape(n, n, 3 * flags.shape[0]).astype(BF16)
-    keep = jnp.pad(keep, ((0, 0), (0, 0), (0, 128 - 3 * flags.shape[0]))).reshape(2, n // 2, n, 128)
+    keep = keep.reshape(2, n // 2, n, 3 * flags.shape[0])
     vm = pl.BlockSpec(memory_space=pltpu.VMEM)
     anywhere = pl.BlockSpec(memory_space=pl.ANY)
     dma = pltpu.SemaphoreType.DMA
     rows = pl.pallas_call(
         functools.partial(kernel, n),
-        out_shape=jax.ShapeDtypeStruct((n, 2, 64, 1024), BF16),
+        out_shape=pltpu.VMEM((n, 2, 64, 1024), BF16),
         in_specs=[anywhere, vm, vm, vm, vm],
-        out_specs=anywhere,
+        out_specs=vm,
         scratch_shapes=[
             pltpu.VMEM((64, 39 * 512), BF16),
             pltpu.VMEM((512, 512), BF16),
             pltpu.VMEM((2048, 128), F32),
             pltpu.VMEM((3, n, 2, n // 2, 8, 128), BF16),
             pltpu.VMEM((3, 2, n, n // 2, 8, 128), BF16),
-            pltpu.VMEM((2, n // 2, n, 128), BF16),
+            pltpu.VMEM((2, n // 2, n, 3 * flags.shape[0]), BF16),
             pltpu.VMEM((3, n * n, 128), F32),
             pltpu.VMEM((8, 768, 128), BF16),
             pltpu.VMEM((8, 256, 768), BF16),

time: 150 us -> 141 us (0.940)
  Pallas kernels: 140 us -> 134 us
  other arithmetic: 7.63 us -> 5.44 us
    pallas_call x1, Pallas kernels: 140 us -> 134 us  [shards(): pl.pallas_call(functools.partial(kernel, n), out_shape=pltpu.VMEM((n, 2,...]
    convert_element_type x1, other arithmetic: 6.66 us -> 4.47 us  [shards(): return rows.astype(F32)]
where the time goes in v3:
time: 141 us
  Pallas kernels  134 us (95%)
  other arithmetic  5.44 us (4%)
    pallas_call x1, Pallas kernels, shards(): pl.pallas_call(functools.partial(kernel, n), out_shape=pltpu.VMEM((n, 2,...  134 us
    convert_element_type x1, other arithmetic, shards(): return rows.astype(F32)  4.47 us

profile of v3, /device:TPU:4, one launch (start us, length us, event | category | flops | bytes accessed | tf_op | source)
XLA Modules:
  0.0 140.6 jit_solution(12498177496124432587)
XLA Ops:
  0.0 1.0 convert_bitcast_fusion
  1.0 0.2 copy.7
  1.2 0.8 convert_element_type.15.mask_ref
  1.9 134.2 %correlate.1 = bf16[16,2,64,1024]{3,2,1,0:T(8,128)(2,1)S(1)} custom-call(bf16[64,12288]{1,0:T(8,128)(2,1)} %v_ref.1, f32[16,512]{1,0:T(8,128)} %taps_ref.1, bf16[512,512]{1,0:T(8,128)(2,1)} %constant.4.clone.tab_ref, bf16[2,8,16,96]{3,2,1,0:T(8,128)(2,1)} %convert_element_type.15.mask_ref, bf16[3,96,128]{2,1,0:T(8,128)(2,1)} %constant.5.clone.spread_ref), custom_call_target="tpu_custom_call" | custom-call | tf_op jit(solution)/shard_map/correlate/pallas_call | solution.py:342
  136.1 4.5 %convert_element_type.16 = f32[16,2,64,1024]{3,2,1,0:T(8,128)} convert(bf16[16,2,64,1024]{3,2,1,0:T(8,128)(2,1)S(1)} %correlate.1) | non-fusion elementwise | flops 2097152 | bytes 12582912 | tf_op jit(solution)/shard_map/convert_element_type | solution.py:369

commit v4 on v3

--- a/solution.py
+++ b/solution.py
@@ -34,9 +34,9 @@
 
 def kernel(
     n,
-    v_ref, taps_ref, tab_ref, mask_ref, spread_ref,
+    v_ref, taps_ref, tab_ref, flags_ref, spread_ref,
     o_ref,
-    ext, filt, w32, wb, rx, mk, mx, zo, lt, zr, ob, mb,
+    fcol, mask_ref, ext, filt, w32, wb, rx, mk, mx, zo, lt, zr, ob, mb,
     vsem, hsend, hrecv, msend, mrecv, xsend, xrecv, zsend, zrecv, osend, orecv, bsend, brecv, lsem, olsem,
 ):
     ci = lax.axis_index("chan")
@@ -186,6 +186,14 @@
                 y = jnp.where(row < 4, y, -y).reshape(128, 128)
                 lt[q, 0:128, r0 : r0 + 128] = b.T.astype(BF16)
                 lt[q, 128:256, r0 : r0 + 128] = y.T.astype(BF16)
+
+    stations = flags_ref.shape[0]
+    for c in range(n):
+        fcol[...] = flags_ref[:, c, :].astype(F32).T
+        for fb in range(3):
+            mask_ref[c // (n // 2), c % (n // 2), :, fb * stations : (fb + 1) * stations] = fcol[
+                pl.ds(fb, n, stride=3), :
+            ].astype(BF16)
 
     load.wait()
     fir(2)
@@ -297,9 +305,6 @@
     pass_on(3, 1)
     pass_on(2, 0)
     step(3)
-    pass_on(3, 0)
-    step(4)
-
     @pl.when(ci < n - 1)
     def _():
         hcopy(0).wait_send()
@@ -311,6 +316,10 @@
     def _(e):
         for fb in range(3):
             xcopy(fb, e).wait_send()
+
+    pass_on(3, 0)
+    step(4)
+
 
     for way in range(2):
         for s in range(4):
@@ -334,8 +343,6 @@
     n = lax.axis_size("stn")
     table = jnp.asarray(dft_table(pfb_taps.shape[1]))
     hot = jnp.asarray(spread(flags.shape[0], 3, 128))
-    keep = jnp.transpose(flags, (1, 2, 0)).reshape(n, n, 3 * flags.shape[0]).astype(BF16)
-    keep = keep.reshape(2, n // 2, n, 3 * flags.shape[0])
     vm = pl.BlockSpec(memory_space=pltpu.VMEM)
     anywhere = pl.BlockSpec(memory_space=pl.ANY)
     dma = pltpu.SemaphoreType.DMA
@@ -345,6 +352,8 @@
         in_specs=[anywhere, vm, vm, vm, vm],
         out_specs=vm,
         scratch_shapes=[
+            pltpu.VMEM((48, flags.shape[0]), F32),
+            pltpu.VMEM((2, n // 2, n, 3 * flags.shape[0]), BF16),
             pltpu.VMEM((64, 39 * 512), BF16),
             pltpu.VMEM((512, 512), BF16),
             pltpu.VMEM((2048, 128), F32),
@@ -365,7 +374,7 @@
             collective_id=0, has_side_effects=True, vmem_limit_bytes=56 << 20
         ),
         name="correlate",
-    )(voltages, pfb_taps, table, keep, hot)
+    )(voltages, pfb_taps, table, flags, hot)
     return rows.astype(F32)
 
 

time: 141 us -> 138 us (0.979)
  no operation moved by 1% of the time
where the time goes in v4:
time: 138 us
  Pallas kernels  134 us (97%)
  other arithmetic  4.47 us (3%)
    pallas_call x1, Pallas kernels, shards(): pl.pallas_call(functools.partial(kernel, n), out_shape=pltpu.VMEM((n, 2,...  134 us
    convert_element_type x1, other arithmetic, shards(): return rows.astype(F32)  4.47 us

profile of v4, /device:TPU:4, one launch (start us, length us, event | category | flops | bytes accessed | tf_op | source)
XLA Modules:
  0.0 138.0 jit_solution(5207907256869434693)
XLA Ops:
  0.0 133.5 %correlate.1 = bf16[16,2,64,1024]{3,2,1,0:T(8,128)(2,1)S(1)} custom-call(bf16[64,12288]{1,0:T(8,128)(2,1)} %v_ref.1, f32[16,512]{1,0:T(8,128)} %taps_ref.1, bf16[512,512]{1,0:T(8,128)(2,1)} %constant.4.clone.tab_ref, s32[32,16,48]{2,1,0:T(8,128)} %flags_ref.1, bf16[3,96,128]{2,1,0:T(8,128)(2,1)} %constant.5.clone.spread_ref), custom_call_target="tpu_custom_call" | custom-call | tf_op jit(solution)/shard_map/correlate/pallas_call | solution.py:349
  133.5 4.5 %convert_element_type.3 = f32[16,2,64,1024]{3,2,1,0:T(8,128)} convert(bf16[16,2,64,1024]{3,2,1,0:T(8,128)(2,1)S(1)} %correlate.1) | non-fusion elementwise | flops 2097152 | bytes 12582912 | tf_op jit(solution)/shard_map/convert_element_type | solution.py:378

commit v5 on v4

--- a/solution.py
+++ b/solution.py
@@ -34,10 +34,10 @@
 
 def kernel(
     n,
-    v_ref, taps_ref, tab_ref, flags_ref, spread_ref,
+    v_ref, taps_in, tab_in, flags_in, spread_in,
     o_ref,
-    fcol, mask_ref, ext, filt, w32, wb, rx, mk, mx, zo, lt, zr, ob, mb,
-    vsem, hsend, hrecv, msend, mrecv, xsend, xrecv, zsend, zrecv, osend, orecv, bsend, brecv, lsem, olsem,
+    taps_ref, tab_ref, flags_ref, spread_ref, fcol, mask_ref, ext, filt, w32, wb, rx, mk, mx, zo, lt, zr, ob, mb,
+    vsem, hsend, hrecv, msend, mrecv, xsend, xrecv, zsend, zrecv, osend, orecv, bsend, brecv, lsem, olsem, isem,
 ):
     ci = lax.axis_index("chan")
     sk = lax.axis_index("stn")
@@ -51,22 +51,28 @@
     def at(dz, hh):
         return lax.rem(z + dz + planes, planes) * 2 + hh
 
-    load = pltpu.make_async_copy(v_ref, ext.at[:, halo * nfft :], vsem)
-    load.start()
-
     bar = pltpu.get_barrier_semaphore()
 
     def greet(chan, stn):
         pl.semaphore_signal(bar, inc=1, device_id={"chan": chan, "stn": stn}, device_id_type=MESH)
+
+    @pl.loop(0, 2)
+    def _(hh):
+        for dz in (3, -3, 2, -2, 1, -1):
+            greet(ci, at(dz, hh))
 
     @pl.loop(1, 2 * n)
     def _(e):
         greet(lax.rem(ci + e // 2, n), z * 2 + lax.rem(h + e, 2))
 
-    @pl.loop(0, 2)
-    def _(hh):
-        for dz in (1, -1, 2, -2, 3, -3):
-            greet(ci, at(dz, hh))
+    load = pltpu.make_async_copy(v_ref, ext.at[:, halo * nfft :], vsem)
+    load.start()
+    flags_load = pltpu.make_async_copy(flags_in, flags_ref, isem.at[0])
+    taps_load = pltpu.make_async_copy(taps_in, taps_ref, isem.at[1])
+    tab_load = pltpu.make_async_copy(tab_in, tab_ref, isem.at[2])
+    spread_load = pltpu.make_async_copy(spread_in, spread_ref, isem.at[3])
+    for each in (flags_load, taps_load, tab_load, spread_load):
+        each.start()
 
     def fir(fb):
         @pl.loop(0, 16)
@@ -187,6 +193,7 @@
                 lt[q, 0:128, r0 : r0 + 128] = b.T.astype(BF16)
                 lt[q, 128:256, r0 : r0 + 128] = y.T.astype(BF16)
 
+    flags_load.wait()
     stations = flags_ref.shape[0]
     for c in range(n):
         fcol[...] = flags_ref[:, c, :].astype(F32).T
@@ -196,7 +203,10 @@
             ].astype(BF16)
 
     load.wait()
+    taps_load.wait()
     fir(2)
+    tab_load.wait()
+    spread_load.wait()
     dft(2)
     pl.semaphore_wait(bar, 2 * n - 1 + 12)
 
@@ -349,9 +359,13 @@
     rows = pl.pallas_call(
         functools.partial(kernel, n),
         out_shape=pltpu.VMEM((n, 2, 64, 1024), BF16),
-        in_specs=[anywhere, vm, vm, vm, vm],
+        in_specs=[anywhere] * 5,
         out_specs=vm,
         scratch_shapes=[
+            pltpu.VMEM(pfb_taps.shape, F32),
+            pltpu.VMEM(table.shape, BF16),
+            pltpu.VMEM(flags.shape, jnp.int32),
+            pltpu.VMEM(hot.shape, BF16),
             pltpu.VMEM((48, flags.shape[0]), F32),
             pltpu.VMEM((2, n // 2, n, 3 * flags.shape[0]), BF16),
             pltpu.VMEM((64, 39 * 512), BF16),
@@ -368,7 +382,7 @@
             pltpu.VMEM((2, 3, 2, 4, 2, 64, 128), BF16),
             dma, dma((2,)), dma((2,)), dma, dma, dma((3, 2 * n)), dma((3, 2 * n)),
             dma((2, 4, 3)), dma((2, 4, 3)), dma((2, 5)), dma((2, 5)),
-            dma((2, 3, 2)), dma((2, 3, 2)), dma((4,)), dma((2, 5)),
+            dma((2, 3, 2)), dma((2, 3, 2)), dma((4,)), dma((2, 5)), dma((4,)),
         ],
         compiler_params=pltpu.CompilerParams(
             collective_id=0, has_side_effects=True, vmem_limit_bytes=56 << 20

time: 138 us -> 137 us (level)
  Pallas kernels: 134 us -> 132 us
    pallas_call x1, Pallas kernels: 134 us -> 132 us  [shards(): pl.pallas_call(functools.partial(kernel, n), out_shape=pltpu.VMEM((n, 2,...]
where the time goes in v5:
time: 137 us
  Pallas kernels  132 us (96%)
  other arithmetic  4.47 us (3%)
    pallas_call x1, Pallas kernels, shards(): pl.pallas_call(functools.partial(kernel, n), out_shape=pltpu.VMEM((n, 2,...  132 us
    convert_element_type x1, other arithmetic, shards(): return rows.astype(F32)  4.47 us

profile of v5, /device:TPU:4, one launch (start us, length us, event | category | flops | bytes accessed | tf_op | source)
XLA Modules:
  0.0 136.6 jit_solution(6234323656970118260)
XLA Ops:
  0.0 132.1 %correlate.1 = bf16[16,2,64,1024]{3,2,1,0:T(8,128)(2,1)S(1)} custom-call(bf16[64,12288]{1,0:T(8,128)(2,1)} %v_ref.1, f32[16,512]{1,0:T(8,128)} %taps_in.1, bf16[512,512]{1,0:T(8,128)(2,1)} %constant.4.clone.tab_in, s32[32,16,48]{2,1,0:T(8,128)} %flags_in.1, bf16[3,96,128]{2,1,0:T(8,128)(2,1)} %constant.5.clone.spread_in), custom_call_target="tpu_custom_call" | custom-call | tf_op jit(solution)/shard_map/correlate/pallas_call | solution.py:359
  132.2 4.5 %convert_element_type.3 = f32[16,2,64,1024]{3,2,1,0:T(8,128)} convert(bf16[16,2,64,1024]{3,2,1,0:T(8,128)(2,1)S(1)} %correlate.1) | non-fusion elementwise | flops 2097152 | bytes 12582912 | tf_op jit(solution)/shard_map/convert_element_type | solution.py:392

commit v6 on v5

--- a/solution.py
+++ b/solution.py
@@ -36,7 +36,7 @@
     n,
     v_ref, taps_in, tab_in, flags_in, spread_in,
     o_ref,
-    taps_ref, tab_ref, flags_ref, spread_ref, fcol, mask_ref, ext, filt, w32, wb, rx, mk, mx, zo, lt, zr, ob, mb,
+    early, taps_ref, tab_ref, flags_ref, spread_ref, fcol, mask_ref, ext, filt, w32, wb, rx, mk, mx, zo, lt, zr, ob, mb,
     vsem, hsend, hrecv, msend, mrecv, xsend, xrecv, zsend, zrecv, osend, orecv, bsend, brecv, lsem, olsem, isem,
 ):
     ci = lax.axis_index("chan")
@@ -283,7 +283,11 @@
         @pl.loop(0, 4)
         def _(q):
             block = zo[way * 4 + q] if s == 0 else zr[way, s - 1, q]
-            o = jnp.dot(lt[way * 4 + q], block, preferred_element_type=F32) * scale
+            if s == 4:
+                o = jnp.dot(lt[way * 4 + q, :, 0:256], block[0:256], preferred_element_type=F32)
+                o = (o + early[way, q]) * scale
+            else:
+                o = jnp.dot(lt[way * 4 + q], block, preferred_element_type=F32) * scale
             rows = o.astype(BF16).reshape(2, 2, 64, 128)
             for p in range(2):
                 for hh in range(2):
@@ -326,6 +330,14 @@
     def _(e):
         for fb in range(3):
             xcopy(fb, e).wait_send()
+
+    for way in range(2):
+
+        @pl.loop(0, 4)
+        def _(q):
+            early[way, q] = jnp.dot(
+                lt[way * 4 + q, :, 256:768], zr[way, 3, q, 256:768, :], preferred_element_type=F32
+            )
 
     pass_on(3, 0)
     step(4)
@@ -362,6 +374,7 @@
         in_specs=[anywhere] * 5,
         out_specs=vm,
         scratch_shapes=[
+            pltpu.VMEM((2, 4, 256, 128), F32),
             pltpu.VMEM(pfb_taps.shape, F32),
             pltpu.VMEM(table.shape, BF16),
             pltpu.VMEM(flags.shape, jnp.int32),

time: 137 us -> 137 us (level)
  no operation moved by 1% of the time
where the time goes in v6:
time: 137 us
  Pallas kernels  132 us (96%)
  other arithmetic  4.47 us (3%)
    pallas_call x1, Pallas kernels, shards(): pl.pallas_call(functools.partial(kernel, n), out_shape=pltpu.VMEM((n, 2,...  132 us
    convert_element_type x1, other arithmetic, shards(): return rows.astype(F32)  4.47 us

profile of v6, /device:TPU:4, one launch (start us, length us, event | category | flops | bytes accessed | tf_op | source)
XLA Modules:
  0.0 136.6 jit_solution(12851139363708382335)
XLA Ops:
  0.0 132.1 %correlate.1 = bf16[16,2,64,1024]{3,2,1,0:T(8,128)(2,1)S(1)} custom-call(bf16[64,12288]{1,0:T(8,128)(2,1)} %v_ref.1, f32[16,512]{1,0:T(8,128)} %taps_in.1, bf16[512,512]{1,0:T(8,128)(2,1)} %constant.4.clone.tab_in, s32[32,16,48]{2,1,0:T(8,128)} %flags_in.1, bf16[3,96,128]{2,1,0:T(8,128)(2,1)} %constant.5.clone.spread_in), custom_call_target="tpu_custom_call" | custom-call | tf_op jit(solution)/shard_map/correlate/pallas_call | solution.py:371
  132.2 4.5 %convert_element_type.3 = f32[16,2,64,1024]{3,2,1,0:T(8,128)} convert(bf16[16,2,64,1024]{3,2,1,0:T(8,128)(2,1)S(1)} %correlate.1) | non-fusion elementwise | flops 2097152 | bytes 12582912 | tf_op jit(solution)/shard_map/convert_element_type | solution.py:405
